TPU v7x, 128 devices: a whole 4x4x4 slice. The times are simulated.
128 devices in a mesh: band: 32 (over y, z, core), lon: 4 (over x).
Axes of the slice: x: 4, y: 4, z: 4, core: 2. Of those that a mesh axis runs over, the one named last changes fastest.
Arguments:
- jacobian: bfloat16 [1048576, 137], P(('band', 'lon')), may hold values from -3 to 3
- departure: float32 [1048576], P(('band', 'lon')), may hold values from -6 to 6
- inv_var: float32 [1048576], P(('band', 'lon')), may hold values from 0.25 to 4
- frac: float32 [2, 1048576], P(None, ('band', 'lon')), may hold values from 0 to 1
- anchors: int32 [2, 1048576], P(None, ('band', 'lon')), may hold values from 0 to 1023, as said below
- counts: int32 [128, 128], P(('band', 'lon')), may hold values from 0 to 64, as said below
Outputs:
- increments: float32 [137, 1024, 512], P(None, 'band', 'lon')
Inputs may be any that keep to these rules, and one draw needn't show every extreme that they name: counts[p, q] is the number of live slots among the 64 that device p holds for owner q; some pairs reach 64 in every draw, and in every draw some owner receives 64 live slots from every device. `anchors`: every slot that device p holds for owner q has its anchor in owner q's block of 32 latitude rows and 128 longitudes, and its latitude row is at most 1022.
All inputs are finite; a program needn't handle non-finite values.
Results may differ from a plain program's by a relative error of at most 0.0041.
Values may be sent and summed in bfloat16 or wider, within the bound.
A program may use at most 64 MiB of HBM per device.

v0:
```python
import math

import jax
import jax.numpy as jnp
from jax import lax
from jax.sharding import PartitionSpec as P

LAT_DEV = 32
LON_DEV = 128


def from_behind(shard, axis, by):
    length = lax.axis_size(axis)
    return lax.ppermute(shard, axis, [(i, (i + by) % length) for i in range(length)])


def shifted(value, axis, steps):
    count = lax.axis_size(axis)
    initial, last = (max(0, -steps), min(count, count - steps))
    return lax.ppermute(value, axis, [(source, source + steps) for source in range(initial, last)])


def block_sums(received, slot_info, first_row, block_rows):
    adjoint_rows = lax.dynamic_slice_in_dim(received, first_row, block_rows, 0)
    row_info = lax.dynamic_slice_in_dim(slot_info, first_row, block_rows, 0)
    lat_local = row_info[:, 4].astype(jnp.int32)
    lon_local = row_info[:, 5].astype(jnp.int32)
    lat_cells = jnp.arange(LAT_DEV + 1, dtype=jnp.int32)
    lon_cells = jnp.arange(LON_DEV, dtype=jnp.int32)
    lat_first = (lat_local[:, None] == lat_cells[None, :]).astype(jnp.bfloat16)
    lat_second = (lat_local[:, None] + 1 == lat_cells[None, :]).astype(jnp.bfloat16)
    lon_first = lon_local[:, None] == lon_cells[None, :]
    lon_second = lon_local[:, None] + 1 == lon_cells[None, :]
    near_row = jnp.where(lon_first, row_info[:, 0:1], 0) + jnp.where(
        lon_second, row_info[:, 1:2], 0
    )
    far_row = jnp.where(lon_first, row_info[:, 2:3], 0) + jnp.where(lon_second, row_info[:, 3:4], 0)
    one_hot = (
        lat_first[:, :, None] * near_row[:, None, :] + lat_second[:, :, None] * far_row[:, None, :]
    )
    one_hot = one_hot.reshape(block_rows, (LAT_DEV + 1) * LON_DEV)
    on_edge = lon_local == LON_DEV - 1
    rim_weight = (
        lat_first * jnp.where(on_edge, row_info[:, 1], 0)[:, None]
        + lat_second * jnp.where(on_edge, row_info[:, 3], 0)[:, None]
    )
    numbers = (((0,), (0,)), ((), ()))
    main_part = lax.dot_general(adjoint_rows, one_hot, numbers, preferred_element_type=jnp.float32)
    rim_part = lax.dot_general(
        adjoint_rows, rim_weight, numbers, preferred_element_type=jnp.float32
    )
    return (main_part, rim_part)


def per_device(jacobian, departure, inv_var, frac, anchors, counts):
    row_total = jacobian.shape[0]
    levels = jacobian.shape[1]
    devices = counts.shape[1]
    capacity = row_total // devices
    lon_count = lax.axis_size("lon")
    within = jnp.arange(capacity, dtype=jnp.int32)
    is_live = (within[None, :] < counts[0][:, None]).reshape(row_total)
    owners = jnp.arange(devices, dtype=jnp.int32)
    lat_start = owners // lon_count * LAT_DEV
    lon_start = owners % lon_count * LON_DEV
    lat_local = (anchors[0].reshape(devices, capacity) - lat_start[:, None]).reshape(row_total)
    lon_local = (anchors[1].reshape(devices, capacity) - lon_start[:, None]).reshape(row_total)
    forcing = departure * inv_var
    adjoint = jnp.where(
        is_live[:, None], forcing[:, None] * jacobian.astype(jnp.float32), 0.0
    ).astype(jnp.bfloat16)
    lat_frac = frac[0]
    lon_frac = frac[1]
    corner_exprs = [
        (1.0 - lat_frac) * (1.0 - lon_frac),
        (1.0 - lat_frac) * lon_frac,
        lat_frac * (1.0 - lon_frac),
        lat_frac * lon_frac,
    ]
    columns = [jnp.where(is_live, value, 0.0) for value in corner_exprs]
    columns = columns + [
        jnp.where(is_live, lat_local, 0).astype(jnp.float32),
        jnp.where(is_live, lon_local, 0).astype(jnp.float32),
    ]
    slot_info = jnp.stack(columns, axis=1).astype(jnp.bfloat16)
    received, row_data = (
        lax.all_to_all(adjoint, ("band", "lon"), split_axis=0, concat_axis=0, tiled=True),
        lax.all_to_all(slot_info, ("band", "lon"), split_axis=0, concat_axis=0, tiled=True),
    )
    block_rows = math.gcd(row_total, 1024)
    main_zero = jnp.zeros((levels, (LAT_DEV + 1) * LON_DEV), jnp.float32)
    rim_zero = jnp.zeros((levels, LAT_DEV + 1), jnp.float32)

    def compute_block(first_row):
        return block_sums(received, row_data, first_row, block_rows)

    def add_block(loop_index, totals):
        first_row = loop_index * block_rows
        main_part, rim_part = compute_block(first_row)
        return (totals[0] + main_part, totals[1] + rim_part)

    main_sum, rim_sum = lax.fori_loop(0, row_total // block_rows, add_block, (main_zero, rim_zero))
    grid_sum = main_sum.reshape(levels, LAT_DEV + 1, LON_DEV)
    from_west = from_behind(rim_sum, "lon", 1)
    grid_sum = grid_sum.at[:, :, 0].add(from_west)
    from_south = shifted(grid_sum[:, LAT_DEV, :], "band", 1)
    return grid_sum[:, :LAT_DEV, :].at[:, 0, :].add(from_south)


def solution(mesh):
    return jax.shard_map(
        per_device,
        mesh=mesh,
        in_specs=(
            P(("band", "lon"), None),
            P(("band", "lon")),
            P(("band", "lon")),
            P(None, ("band", "lon")),
            P(None, ("band", "lon")),
            P(("band", "lon"), None),
        ),
        out_specs=P(None, "band", "lon"),
        check_vma=False,
    )
```

profile of v0, /device:TPU:1, one launch (start us, length us, event | category | flops | bytes accessed | tf_op | source)
XLA Modules:
  0.0 187.4 jit_solution(9416513923101126369)
XLA Ops:
  0.0 1.1 slice_reduce_fusion.3
  1.3 1.1 slice_reduce_fusion
  2.5 0.7 fusion.25
  3.2 0.7 fusion.26
  4.0 0.7 fusion.27
  4.7 0.7 fusion.28
  5.5 0.8 fusion.29
  6.3 0.8 fusion.30
  7.2 0.9 reshape.716
  8.1 11.5 %all-to-all-start.1 = ((bf16[128,2,192]{2,1,0:T(2,128)(2,1)}), bf16[128,2,192]{2,1,0:T(2,128)(2,1)S(1)}, u32[]{:S(2)}, u32[]{:S(2)}) async-start(bf16[128,2,192]{2,1,0:T(2,128)(2,1)} %reshape.716), calls=%async_computation.1 | async-start | bytes 262144 | tf_op jit(solution)/shard_map/all_to_all | solution.py:88
  19.6 0.7 iota_compare_fusion.5
  20.4 0.8 mul.221
  21.2 2.3 %select_convert_fusion = bf16[8192,137]{0,1:T(8,128)(2,1)S(1)} fusion(bf16[8192,137]{0,1:T(8,128)(2,1)} %param.12, f32[8192]{0:T(1024)S(1)} %mul.221, pred[8192]{0:T(1024)(128)(4,1)S(1)} %lt.89), kind=kLoop, calls=%fused_computation.40 | loop fusion | flops 4489216 | bytes 4530176 | tf_op jit(solution)/shard_map/convert_element_type | solution.py:71
  23.4 3.9 %copy.23 = bf16[8192,137]{1,0:T(8,128)(2,1)} copy(bf16[8192,137]{0,1:T(8,128)(2,1)S(1)} %select_convert_fusion) | data formatting | bytes 4489216 | tf_op jit(solution)/shard_map/all_to_all | solution.py:87
  27.3 2.3 %all-to-all-done.1 = bf16[128,2,192]{2,1,0:T(2,128)(2,1)S(1)} async-done(((bf16[128,2,192]{2,1,0:T(2,128)(2,1)}), bf16[128,2,192]{2,1,0:T(2,128)(2,1)S(1)}, u32[]{:S(2)}, u32[]{:S(2)}) %all-to-all-start.1) | async-done | bytes 98336 | tf_op jit(solution)/shard_map/all_to_all | solution.py:88
  29.6 7.9 %all-to-all-start = ((bf16[128,64,137]{2,1,0:T(8,128)(2,1)}), bf16[128,64,137]{2,1,0:T(8,128)(2,1)}, u32[]{:S(2)}, u32[]{:S(2)}) async-start(bf16[128,64,137]{2,1,0:T(8,128)(2,1)} %bitcast.33), calls=%async_computation | async-start | bytes 8388608 | tf_op jit(solution)/shard_map/all_to_all | solution.py:87
  37.6 0.2 reshape.717
  37.8 0.2 all_to_all.18
  38.0 52.6 %all-to-all-done = bf16[128,64,137]{2,1,0:T(8,128)(2,1)} async-done(((bf16[128,64,137]{2,1,0:T(8,128)(2,1)}), bf16[128,64,137]{2,1,0:T(8,128)(2,1)}, u32[]{:S(2)}, u32[]{:S(2)}) %all-to-all-start) | async-done | bytes 2244640 | tf_op jit(solution)/shard_map/all_to_all | solution.py:87
  90.6 62.2 %while.20 = (s32[]{:T(128)}, f32[137,4224]{1,0:T(8,128)S(1)}, f32[137,33]{0,1:T(8,128)S(1)}, bf16[8192,137]{1,0:T(8,128)(2,1)}, bf16[8192,6]{0,1:T(8,128)(2,1)S(...) while((s32[]{:T(128)}, f32[137,4224]{1,0:T(8,128)S(1)}, ...), condition=%wide.region_1.2_spmd.clone, body=%wide.region_0.1_spmd.clone.sunk | while | flops 1210802304 | bytes 24416876 | solution.py:102
  90.7 0.1 fusion.45
  90.9 1.2 convolution_add_fusion.5
  92.2 0.2 fusion.46
  92.3 1.2 multiply_add_fusion.2
  93.5 4.9 %convolution_add_fusion.4 = f32[137,4224]{1,0:T(8,128)S(1)} fusion(bf16[1024,4224]{0,1:T(8,128)(2,1)S(1)} %bitcast.32, f32[137,4224]{1,0:T(8,128)S(1)} %get-tuple-element.296, pred[]{:T(512)S(6)} %compare.20, bf16[8192,137]{1,0:T(8,128)(2,1)} %get-tuple-element.312, s32[]{:T(128)S(6)} %select_n.249), kind=kOutput, calls=%fused_computation.1.clone.1 | convolution fusion | flops 1186310400 | bytes 13804549 | tf_op jit(solution)/shard_map/while/body/eval_jaxpr/dot_general | solution.py:48
  98.6 1.2 convolution_add_fusion.5
  99.9 0.2 fusion.46
  100.1 1.2 multiply_add_fusion.2
  101.3 4.9 %convolution_add_fusion.4 = f32[137,4224]{1,0:T(8,128)S(1)} fusion(bf16[1024,4224]{0,1:T(8,128)(2,1)S(1)} %bitcast.32, f32[137,4224]{1,0:T(8,128)S(1)} %get-tuple-element.296, pred[]{:T(512)S(6)} %compare.20, bf16[8192,137]{1,0:T(8,128)(2,1)} %get-tuple-element.312, s32[]{:T(128)S(6)} %select_n.249), kind=kOutput, calls=%fused_computation.1.clone.1 | convolution fusion | flops 1186310400 | bytes 13804549 | tf_op jit(solution)/shard_map/while/body/eval_jaxpr/dot_general | solution.py:48
  106.2 0.1 fusion.45
  106.4 1.2 convolution_add_fusion.5
  107.7 0.2 fusion.46
  107.9 1.2 multiply_add_fusion.2
  109.0 4.9 %convolution_add_fusion.4 = f32[137,4224]{1,0:T(8,128)S(1)} fusion(bf16[1024,4224]{0,1:T(8,128)(2,1)S(1)} %bitcast.32, f32[137,4224]{1,0:T(8,128)S(1)} %get-tuple-element.296, pred[]{:T(512)S(6)} %compare.20, bf16[8192,137]{1,0:T(8,128)(2,1)} %get-tuple-element.312, s32[]{:T(128)S(6)} %select_n.249), kind=kOutput, calls=%fused_computation.1.clone.1 | convolution fusion | flops 1186310400 | bytes 13804549 | tf_op jit(solution)/shard_map/while/body/eval_jaxpr/dot_general | solution.py:48
  114.0 0.1 fusion.45
  114.2 1.2 convolution_add_fusion.5
  115.5 0.2 fusion.46
  115.6 1.2 multiply_add_fusion.2
  116.8 4.9 %convolution_add_fusion.4 = f32[137,4224]{1,0:T(8,128)S(1)} fusion(bf16[1024,4224]{0,1:T(8,128)(2,1)S(1)} %bitcast.32, f32[137,4224]{1,0:T(8,128)S(1)} %get-tuple-element.296, pred[]{:T(512)S(6)} %compare.20, bf16[8192,137]{1,0:T(8,128)(2,1)} %get-tuple-element.312, s32[]{:T(128)S(6)} %select_n.249), kind=kOutput, calls=%fused_computation.1.clone.1 | convolution fusion | flops 1186310400 | bytes 13804549 | tf_op jit(solution)/shard_map/while/body/eval_jaxpr/dot_general | solution.py:48
  122.0 1.2 convolution_add_fusion.5
  123.2 0.2 fusion.46
  123.4 1.2 multiply_add_fusion.2
  124.6 4.9 %convolution_add_fusion.4 = f32[137,4224]{1,0:T(8,128)S(1)} fusion(bf16[1024,4224]{0,1:T(8,128)(2,1)S(1)} %bitcast.32, f32[137,4224]{1,0:T(8,128)S(1)} %get-tuple-element.296, pred[]{:T(512)S(6)} %compare.20, bf16[8192,137]{1,0:T(8,128)(2,1)} %get-tuple-element.312, s32[]{:T(128)S(6)} %select_n.249), kind=kOutput, calls=%fused_computation.1.clone.1 | convolution fusion | flops 1186310400 | bytes 13804549 | tf_op jit(solution)/shard_map/while/body/eval_jaxpr/dot_general | solution.py:48
  129.7 1.2 convolution_add_fusion.5
  131.0 0.2 fusion.46
  131.2 1.2 multiply_add_fusion.2
  132.4 4.9 %convolution_add_fusion.4 = f32[137,4224]{1,0:T(8,128)S(1)} fusion(bf16[1024,4224]{0,1:T(8,128)(2,1)S(1)} %bitcast.32, f32[137,4224]{1,0:T(8,128)S(1)} %get-tuple-element.296, pred[]{:T(512)S(6)} %compare.20, bf16[8192,137]{1,0:T(8,128)(2,1)} %get-tuple-element.312, s32[]{:T(128)S(6)} %select_n.249), kind=kOutput, calls=%fused_computation.1.clone.1 | convolution fusion | flops 1186310400 | bytes 13804549 | tf_op jit(solution)/shard_map/while/body/eval_jaxpr/dot_general | solution.py:48
  137.5 1.2 convolution_add_fusion.5
  138.8 0.2 fusion.46
  139.0 1.2 multiply_add_fusion.2
  140.1 4.9 %convolution_add_fusion.4 = f32[137,4224]{1,0:T(8,128)S(1)} fusion(bf16[1024,4224]{0,1:T(8,128)(2,1)S(1)} %bitcast.32, f32[137,4224]{1,0:T(8,128)S(1)} %get-tuple-element.296, pred[]{:T(512)S(6)} %compare.20, bf16[8192,137]{1,0:T(8,128)(2,1)} %get-tuple-element.312, s32[]{:T(128)S(6)} %select_n.249), kind=kOutput, calls=%fused_computation.1.clone.1 | convolution fusion | flops 1186310400 | bytes 13804549 | tf_op jit(solution)/shard_map/while/body/eval_jaxpr/dot_general | solution.py:48
  145.3 1.2 convolution_add_fusion.5
  146.6 0.2 fusion.46
  146.7 1.2 multiply_add_fusion.2
  147.9 4.9 %convolution_add_fusion.4 = f32[137,4224]{1,0:T(8,128)S(1)} fusion(bf16[1024,4224]{0,1:T(8,128)(2,1)S(1)} %bitcast.32, f32[137,4224]{1,0:T(8,128)S(1)} %get-tuple-element.296, pred[]{:T(512)S(6)} %compare.20, bf16[8192,137]{1,0:T(8,128)(2,1)} %get-tuple-element.312, s32[]{:T(128)S(6)} %select_n.249), kind=kOutput, calls=%fused_computation.1.clone.1 | convolution fusion | flops 1186310400 | bytes 13804549 | tf_op jit(solution)/shard_map/while/body/eval_jaxpr/dot_general | solution.py:48
  152.8 0.4 collective-permute-start
  153.2 1.9 %reshape.683 = f32[137,33,128]{2,1,0:T(8,128)} reshape(f32[137,4224]{1,0:T(8,128)S(1)} %get-tuple-element.162) | data formatting | bytes 4629504 | tf_op jit(solution)/shard_map/reshape | solution.py:103
  155.1 1.8 collective-permute-done
  156.9 3.1 %copy.21 = f32[137,33,1]{2,1,0:T(8,128)} copy(f32[137,33,1]{0,1,2:T(8,128)S(1)} %bitcast.44) | data formatting | bytes 36168 | tf_op jit(solution)/shard_map/reshape.45
  160.0 3.7 %slice_add_fusion = f32[137,33,1]{2,1,0:T(8,128)} fusion(f32[137,33,1]{2,1,0:T(8,128)} %copy.21, f32[137,33,128]{2,1,0:T(8,128)S(1)} %copy-done), kind=kLoop, calls=%fused_computation.41 | loop fusion | flops 4521 | bytes 54252 | tf_op jit(solution)/shard_map/add | solution.py:105
  163.7 14.7 %scatter-add.6 = f32[137,33,128]{2,1,0:T(8,128)S(1)} dynamic-update-slice(f32[137,33,128]{2,1,0:T(8,128)S(1)} %copy-done, f32[137,33,1]{2,1,0:T(8,128)} %slice_add_fusion, s32[]{:T(128)} %constant.147.clone.1, s32[]{:T(128)} %constant.147.clone.1, s32[]{:T(128)} %constant.147.clone.1) | dynamic-update-slice | bytes 36172 | tf_op jit(solution)/shard_map/scatter-add | solution.py:105
  178.4 3.6 %collective-permute-start.1 = (f32[137,128]{1,0:T(8,128)S(1)}, f32[137,128]{1,0:T(8,128)S(1)}, u32[]{:S(2)}, u32[]{:S(2)}) collective-permute-start(f32[137,128]{1,0:T(8,128)S(1)} %bitcast.43), channel_id=1, source_target_pairs={{0,4},{4,8},{8,12},{12,16},{16,20},{20,24},{24,28},{28,32},{32,36}... | collective-permute-start | bytes 210440 | tf_op jit(solution)/shard_map/ppermute | solution.py:20
  182.1 1.7 slice.140
  183.9 3.5 %scatter-add.9 = f32[137,32,128]{2,1,0:T(8,128)} dynamic-update-slice(f32[137,32,128]{2,1,0:T(8,128)} %slice.140, f32[137,1,128]{2,1,0:T(1,128)S(1)} %slice_add_fusion.1, s32[]{:T(128)} %constant.147.clone.1, s32[]{:T(128)} %constant.147.clone.1, s32[]{:T(128)} %constant.147.clone.1) | dynamic-update-slice | bytes 140292 | tf_op jit(solution)/shard_map/scatter-add | solution.py:107
  (46 shorter events, 2.5 us)
Async XLA Ops:
  8.1 21.5 %all-to-all-start.1 = ((bf16[128,2,192]{2,1,0:T(2,128)(2,1)}), bf16[128,2,192]{2,1,0:T(2,128)(2,1)S(1)}, u32[]{:S(2)}, u32[]{:S(2)}) async-start(bf16[128,2,192]{2,1,0:T(2,128)(2,1)} %reshape.716), calls=%async_computation.1 | async-start | bytes 262144 | tf_op jit(solution)/shard_map/all_to_all | solution.py:88
  29.6 61.0 %all-to-all-start = ((bf16[128,64,137]{2,1,0:T(8,128)(2,1)}), bf16[128,64,137]{2,1,0:T(8,128)(2,1)}, u32[]{:S(2)}, u32[]{:S(2)}) async-start(bf16[128,64,137]{2,1,0:T(8,128)(2,1)} %bitcast.33), calls=%async_computation | async-start | bytes 8388608 | tf_op jit(solution)/shard_map/all_to_all | solution.py:87
  152.8 4.1 %collective-permute-start = (f32[137,33]{0,1:T(8,128)S(1)}, f32[137,33]{0,1:T(8,128)S(1)}, u32[]{:S(2)}, u32[]{:S(2)}) collective-permute-start(f32[137,33]{0,1:T(8,128)S(1)} %get-tuple-element.163), channel_id=1, source_target_pairs={{0,1},{1,2},{2,3},{3,0},{4,5},{5,6},{6,7},{7,4},{8,9},{9,10},{10,1... | collective-permute-start | bytes 54260 | tf_op jit(solution)/shard_map/ppermute | solution.py:14
  155.1 4.9 %copy-start = (f32[137,33,128]{2,1,0:T(8,128)S(1)}, f32[137,33,128]{2,1,0:T(8,128)}, u32[]{:S(2)}) copy-start(f32[137,33,128]{2,1,0:T(8,128)} %reshape.683) | copy-start | bytes 6944260
  178.4 5.3 %collective-permute-start.1 = (f32[137,128]{1,0:T(8,128)S(1)}, f32[137,128]{1,0:T(8,128)S(1)}, u32[]{:S(2)}, u32[]{:S(2)}) collective-permute-start(f32[137,128]{1,0:T(8,128)S(1)} %bitcast.43), channel_id=1, source_target_pairs={{0,4},{4,8},{8,12},{12,16},{16,20},{20,24},{24,28},{28,32},{32,36}... | collective-permute-start | bytes 210440 | tf_op jit(solution)/shard_map/ppermute | solution.py:20
where the time goes:
time: 190 us; the launch traced here: 187 us
  waiting for transfers between devices  56.8 us (30%)
  matrix products  48.8 us (26%)
  local copies, waits for them, and re-layouts  32.7 us (17%)
  other arithmetic  24.9 us (13%)
  starting transfers between devices  23.4 us (12%)
    all_to_all x1, waiting for transfers between devices, per_device(): lax.all_to_all(adjoint, ('band', 'lon'), split_axis=0, concat_axis=0, til...  52.6 us
    dot_general x8, matrix products, block_sums(): lax.dot_general(adjoint_rows, one_hot, numbers, preferred_element_type=jn...  38.9 us
    scatter-add x1, local copies, waits for them, and re-layouts, per_device(): grid_sum = grid_sum.at[:, :, 0].add(from_west)  14.7 us
    all_to_all x1, starting transfers between devices, per_device(): lax.all_to_all(slot_info, ('band', 'lon'), split_axis=0, concat_axis=0, t...  11.5 us
    dot_general x8, matrix products, block_sums(): lax.dot_general(adjoint_rows, rim_weight, numbers, preferred_element_type...  9.94 us
    add x8, other arithmetic, block_sums(): lat_first[:, :, None] * near_row[:, None, :]  9.35 us
    all_to_all x1, starting transfers between devices, per_device(): lax.all_to_all(adjoint, ('band', 'lon'), split_axis=0, concat_axis=0, til...  7.93 us
    all_to_all x1, local copies, waits for them, and re-layouts, per_device(): lax.all_to_all(adjoint, ('band', 'lon'), split_axis=0, concat_axis=0, til...  3.86 us
  transfers between devices with their start and end apart: 4, of which 3 were waited for; matrix products, arithmetic and copies ran while one was open for 6% of the time, Pallas kernels for 0%

commit v1 on v0

v1 whole, which is shorter than its diff:
```python
import functools

import jax
import jax.numpy as jnp
from jax import lax
from jax.experimental import pallas as pl
from jax.experimental.pallas import tpu as pltpu
from jax.sharding import PartitionSpec as P

LEV = 137
LAT_DEV = 32
LON_DEV = 128
CAP = 64
ROWS = 144
HALF = ROWS // 2
GROUPS = 4
GROUP_LAT = LAT_DEV // GROUPS
WIDE = (GROUP_LAT + 2) * LON_DEV
F32 = jnp.float32
BF16 = jnp.bfloat16


def lanes(rows=1):
    return lax.broadcasted_iota(jnp.int32, (rows, 128), 1)


def pack_pair(pair, jac_ref, dep_ref, inv_ref, frac_ref, anch_ref, counts_ref):
    cols = pl.ds(pl.multiple_of(pair * 128, 128), 128)
    lane = lanes()
    first = lane < CAP
    limit = jnp.where(first, counts_ref[0, 2 * pair], counts_ref[0, 2 * pair + 1])
    live = (lane % CAP) < limit
    forcing = dep_ref[pl.ds(pair, 1), :] * inv_ref[pl.ds(pair, 1), :]
    top = jnp.where(live, jac_ref[0:136, cols].astype(F32) * forcing, 0.0)
    last = jnp.where(live, jac_ref[136:137, cols].astype(F32) * forcing, 0.0)
    a = frac_ref[0:1, cols]
    b = frac_ref[1:2, cols]
    lat = (anch_ref[0:1, cols] % LAT_DEV).astype(F32)
    lon = (anch_ref[1:2, cols] % LON_DEV).astype(F32)
    items = [last, (1.0 - a) * (1.0 - b), (1.0 - a) * b, a * (1.0 - b), a * b, lat, lon]
    row = lax.broadcasted_iota(jnp.int32, (8, 128), 0)
    tail = jnp.zeros((8, 128), F32)
    for n, item in enumerate(items):
        tail = jnp.where((row == n) & live, item, tail)
    low = top[0:HALF]
    high = jnp.concatenate([top[HALF:136], tail], axis=0)
    left = lanes(HALF) < CAP
    one = jnp.where(left, low, pltpu.roll(high, CAP, 1))
    two = jnp.where(left, pltpu.roll(low, CAP, 1), high)
    return one.astype(BF16), two.astype(BF16)


def pack_kernel(jac_ref, dep_ref, inv_ref, frac_ref, anch_ref, counts_ref, out_ref):
    def body(pair, carry):
        one, two = pack_pair(pair, jac_ref, dep_ref, inv_ref, frac_ref, anch_ref, counts_ref)
        out_ref[2 * pair] = one
        out_ref[2 * pair + 1] = two
        return carry

    lax.fori_loop(0, 64, body, 0)


def unpack_pair(one, two):
    left = lanes(HALF) < CAP
    one = one.astype(F32)
    two = two.astype(F32)
    low = jnp.where(left, one, pltpu.roll(two, CAP, 1))
    high = jnp.where(left, pltpu.roll(one, CAP, 1), two)
    return jnp.concatenate([low, high], axis=0)


def spread(slots, lhs_ref, rhs_ref, at):
    cols = pl.ds(at, 128)
    info = slots[136:144]
    w00, w01, w10, w11 = (info[n : n + 1] for n in range(1, 5))
    lat, lon = info[5:6], info[6:7]
    group = jnp.floor(lat * (1.0 / GROUP_LAT))
    inner = lat - group * GROUP_LAT
    adj = slots.astype(BF16)
    for h in range(GROUPS):
        mask = jnp.where(group == h, 1.0, 0.0).astype(BF16)
        lhs_ref[h * ROWS : (h + 1) * ROWS, cols] = adj * mask
    j = lax.broadcasted_iota(jnp.int32, (LON_DEV, 128), 0).astype(F32)
    here = j == lon
    after = j == lon + 1.0
    near = jnp.where(here, w00, jnp.where(after, w01, 0.0)).astype(BF16)
    far = jnp.where(here, w10, jnp.where(after, w11, 0.0)).astype(BF16)
    for r in range(GROUP_LAT + 1):
        on_near = jnp.where(inner == r, 1.0, 0.0).astype(BF16)
        on_far = jnp.where(inner + 1.0 == r, 1.0, 0.0).astype(BF16)
        rhs_ref[r * LON_DEV : (r + 1) * LON_DEV, cols] = near * on_near + far * on_far
    edge = lon == LON_DEV - 1.0
    r = lax.broadcasted_iota(jnp.int32, (16, 128), 0).astype(F32)
    rim = jnp.where(edge & (r == inner), w01, jnp.where(edge & (r == inner + 1.0), w11, 0.0))
    rhs_ref[(GROUP_LAT + 1) * LON_DEV : (GROUP_LAT + 1) * LON_DEV + 16, cols] = rim.astype(BF16)


def sum_kernel(depth, recv_ref, acc_ref, lhs_ref, rhs_ref):
    acc_ref[...] = jnp.zeros_like(acc_ref)
    rhs_ref[...] = jnp.zeros_like(rhs_ref)

    def body(step, carry):
        for n in range(depth // 128):
            pair = step * (depth // 128) + n
            spread(unpack_pair(recv_ref[2 * pair], recv_ref[2 * pair + 1]), lhs_ref, rhs_ref, n * 128)
        acc_ref[...] += lax.dot_general(
            lhs_ref[...], rhs_ref[...], (((1,), (1,)), ((), ())), preferred_element_type=F32
        )
        return carry

    lax.fori_loop(0, 8192 // depth, body, 0)


def halo_of(acc):
    east = acc[0, :, -LON_DEV:]
    for h in range(1, GROUPS):
        east = east + jnp.roll(acc[h, :, -LON_DEV:], h * GROUP_LAT, axis=1)
    return east, acc[GROUPS - 1, :, GROUP_LAT * LON_DEV : (GROUP_LAT + 1) * LON_DEV]


def final_kernel(acc_ref, west_ref, north_ref, corner_ref, out_ref):
    rows = acc_ref.shape[1]
    lane = lanes(rows)
    for h in range(GROUPS):
        for r in range(GROUP_LAT):
            i = h * GROUP_LAT + r
            value = acc_ref[h, :, r * LON_DEV : (r + 1) * LON_DEV]
            side = west_ref[:, i : i + 1]
            if r == 0 and h > 0:
                value = value + acc_ref[h - 1, :, GROUP_LAT * LON_DEV : (GROUP_LAT + 1) * LON_DEV]
            if i == 0:
                value = value + north_ref[...]
                side = side + corner_ref[:, LAT_DEV : LAT_DEV + 1]
            value = value + jnp.where(lane == 0, side, 0.0)
            out_ref[pl.ds(i, rows, stride=LAT_DEV), :] = value


def per_device(jacobian, departure, inv_var, frac, anchors, counts):
    vmem = pl.BlockSpec(memory_space=pltpu.VMEM)
    packed = pl.pallas_call(
        pack_kernel,
        out_shape=jax.ShapeDtypeStruct((128, HALF, 128), BF16),
        in_specs=[vmem] * 5 + [pl.BlockSpec(memory_space=pltpu.SMEM)],
        out_specs=vmem,
        name="pack",
    )(jacobian.T, departure.reshape(64, 128), inv_var.reshape(64, 128), frac, anchors, counts)
    received = lax.all_to_all(packed, ("band", "lon"), split_axis=0, concat_axis=0, tiled=True)
    depth = 512
    acc = pl.pallas_call(
        functools.partial(sum_kernel, depth),
        out_shape=jax.ShapeDtypeStruct((GROUPS * ROWS, WIDE), F32),
        in_specs=[vmem],
        out_specs=vmem,
        scratch_shapes=[pltpu.VMEM((GROUPS * ROWS, depth), BF16), pltpu.VMEM((WIDE, depth), BF16)],
        compiler_params=pltpu.CompilerParams(vmem_limit_bytes=40 * 2**20),
        name="sums",
    )(received).reshape(GROUPS, ROWS, WIDE)
    east, south = halo_of(acc)
    bands, lons = lax.axis_size("band"), lax.axis_size("lon")
    to_east = [(i, (i + 1) % lons) for i in range(lons)]
    to_south = [(i, i + 1) for i in range(bands - 1)]
    west = lax.ppermute(east, "lon", to_east)
    north = lax.ppermute(south, "band", to_south)
    corner = lax.ppermute(west, "band", to_south)
    block = 48
    out = pl.pallas_call(
        final_kernel,
        grid=(ROWS // block,),
        out_shape=jax.ShapeDtypeStruct((LEV * LAT_DEV, LON_DEV), F32),
        in_specs=[pl.BlockSpec((GROUPS, block, WIDE), lambda n: (0, n, 0))]
        + [pl.BlockSpec((block, LON_DEV), lambda n: (n, 0))] * 3,
        out_specs=pl.BlockSpec((block * LAT_DEV, LON_DEV), lambda n: (n, 0)),
        name="final",
    )(acc, west, north, corner)
    return out.reshape(LEV, LAT_DEV, LON_DEV)


def solution(mesh):
    return jax.shard_map(
        per_device,
        mesh=mesh,
        in_specs=(
            P(("band", "lon"), None),
            P(("band", "lon")),
            P(("band", "lon")),
            P(None, ("band", "lon")),
            P(None, ("band", "lon")),
            P(("band", "lon"), None),
        ),
        out_specs=P(None, "band", "lon"),
        check_vma=False,
    )
```

time: 190 us -> 93.2 us (0.49)
  the two profiles are of different devices: /device:TPU:1 before, /device:TPU:8 now
where the time goes in v1:
time: 93.2 us; the launch traced here: 92.8 us
  blocking collectives  43 us (46%)
  Pallas kernels  35.2 us (38%)
  waiting for transfers between devices  9.03 us (10%)
  starting transfers between devices  4.54 us (5%)
    all_to_all x1, blocking collectives, per_device(): lax.all_to_all(packed, ('band', 'lon'), split_axis=0, concat_axis=0, tile...  43 us
    pallas_call x1, Pallas kernels, per_device(): pl.pallas_call(functools.partial(sum_kernel, depth), out_shape=jax.ShapeD...  21 us
    pallas_call x1, Pallas kernels, per_device(): pl.pallas_call(pack_kernel, out_shape=jax.ShapeDtypeStruct((128, HALF, 12...  9.31 us
    ppermute x1, waiting for transfers between devices, per_device(): corner = lax.ppermute(west, 'band', to_south)  5.17 us
    pallas_call x1, Pallas kernels, per_device(): pl.pallas_call(final_kernel, grid=(ROWS // block,), out_shape=jax.ShapeDt...  4.94 us
    ppermute x1, waiting for transfers between devices, per_device(): west = lax.ppermute(east, 'lon', to_east)  3.18 us
    ppermute x1, starting transfers between devices, per_device(): north = lax.ppermute(south, 'band', to_south)  1.98 us
    ppermute x1, starting transfers between devices, per_device(): corner = lax.ppermute(west, 'band', to_south)  1.91 us
  transfers between devices with their start and end apart: 3, of which 3 were waited for; matrix products, arithmetic and copies ran while one was open for 0% of the time, Pallas kernels for 0%

profile of v1, /device:TPU:8, one launch (start us, length us, event | category | flops | bytes accessed | tf_op | source)
XLA Modules:
  0.0 92.8 jit_solution(9021565559633740075)
XLA Ops:
  0.0 9.3 %pack.1 = bf16[128,72,128]{2,1,0:T(8,128)(2,1)} custom-call(bf16[137,8192]{1,0:T(8,128)(2,1)} %bitcast.27, f32[64,128]{1,0:T(8,128)} %bitcast.31, f32[64,128]{1,0:T(8,128)} %bitcast.32, f32[2,8192]{1,0:T(2,128)} %frac_ref.1, s32[2,8192]{1,0:T(2,128)} %anch_ref.1, s32[1,128]{1,0:T(1,128)} %counts_ref.1), custom_call_target="tpu_custom_call" | custom-call | tf_op jit(solution)/shard_map/pack/pallas_call | solution.py:140
  9.3 43.0 %all_to_all.5.recv_ref = bf16[128,72,128]{2,1,0:T(8,128)(2,1)S(1)} all-to-all(bf16[128,72,128]{2,1,0:T(8,128)(2,1)} %pack.1), channel_id=1, replica_groups=mesh['band'=32,'lon'=4] {'band','lon'}, dimensions={0} | all-to-all | bytes 4718592 | tf_op jit(solution)/shard_map/all_to_all | solution.py:147
  52.3 21.0 %sums.1 = f32[576,1280]{1,0:T(8,128)S(1)} custom-call(bf16[128,72,128]{2,1,0:T(8,128)(2,1)S(1)} %all_to_all.5.recv_ref), custom_call_target="tpu_custom_call" | custom-call | tf_op jit(solution)/shard_map/sums/pallas_call | solution.py:149
  73.2 0.0 copy-start
  73.3 0.1 slice.58
  73.4 0.1 slice.55
  73.4 0.1 slice.52
  73.5 0.1 fusion.2
  73.7 0.6 collective-permute-start
  74.3 2.0 %collective-permute-start.1 = (f32[144,128]{1,0:T(8,128)S(1)}, f32[144,128]{1,0:T(8,128)S(1)}, u32[]{:S(2)}, u32[]{:S(2)}) collective-permute-start(f32[144,128]{1,0:T(8,128)S(1)} %get-tuple-element.5), channel_id=1, source_target_pairs={{0,4},{4,8},{8,12},{12,16},{16,20},{20,24},{24,28},{28,32},{32,36}... | collective-permute-start | bytes 221192 | tf_op jit(solution)/shard_map/ppermute | solution.py:163
  76.3 3.2 %collective-permute-done.west_ref = f32[144,128]{1,0:T(8,128)S(1)} collective-permute-done((f32[144,128]{1,0:T(8,128)S(1)}, f32[144,128]{1,0:T(8,128)S(1)}, u32[]{:S(2)}, u32[]{:S(2)}) %collective-permute-start) | collective-permute-done | bytes 73760 | tf_op jit(solution)/shard_map/ppermute | solution.py:162
  79.5 0.0 copy-start.1
  79.5 1.9 %collective-permute-start.2 = (f32[144,128]{1,0:T(8,128)S(1)}, f32[144,128]{1,0:T(8,128)S(1)}, u32[]{:S(2)}, u32[]{:S(2)}) collective-permute-start(f32[144,128]{1,0:T(8,128)S(1)} %collective-permute-done.west_ref), channel_id=1, source_target_pairs={{0,4},{4,8},{8,12},{12,16},{16,20},{20,24},{24,28},{28,32},{32,36}... | collective-permute-start | bytes 221192 | tf_op jit(solution)/shard_map/ppermute | solution.py:164
  81.4 0.7 collective-permute-done.1.north_ref
  82.1 0.0 copy-start.2
  82.1 5.2 %collective-permute-done.2.corner_ref = f32[144,128]{1,0:T(8,128)S(1)} collective-permute-done((f32[144,128]{1,0:T(8,128)S(1)}, f32[144,128]{1,0:T(8,128)S(1)}, u32[]{:S(2)}, u32[]{:S(2)}) %collective-permute-start.2) | collective-permute-done | bytes 73760 | tf_op jit(solution)/shard_map/ppermute | solution.py:164
  87.3 0.0 copy-done
  87.3 0.0 copy-done.1
  87.3 0.0 copy-done.2
  87.3 0.0 copy-start.3
  87.3 0.6 copy-done.3
  87.9 4.9 %final.1 = f32[4384,128]{1,0:T(8,128)} custom-call(f32[4,144,1280]{2,1,0:T(8,128)} %bitcast.26, f32[144,128]{1,0:T(8,128)} %copy-done.1, f32[144,128]{1,0:T(8,128)} %copy-done.2, f32[144,128]{1,0:T(8,128)} %copy-done.3), custom_call_target="tpu_custom_call" | custom-call | tf_op jit(solution)/shard_map/final/pallas_call | solution.py:166
  (1 shorter events, 0.0 us)
Async XLA Ops:
  73.2 14.0 %copy-start = (f32[576,1280]{1,0:T(8,128)}, f32[576,1280]{1,0:T(8,128)S(1)}, u32[]{:S(2)}) copy-start(f32[576,1280]{1,0:T(8,128)S(1)} %sums.1) | copy-start | bytes 8847364
  73.7 5.8 %collective-permute-start = (f32[144,128]{1,0:T(8,128)S(1)}, f32[144,128]{1,0:T(8,128)S(1)}, u32[]{:S(2)}, u32[]{:S(2)}) collective-permute-start(f32[144,128]{1,0:T(8,128)S(1)} %fusion.2), channel_id=1, source_target_pairs={{0,1},{1,2},{2,3},{3,0},{4,5},{5,6},{6,7},{7,4},{8,9},{9,10},{10,1... | collective-permute-start | bytes 221192 | tf_op jit(solution)/shard_map/ppermute | solution.py:162
  74.3 7.8 %collective-permute-start.1 = (f32[144,128]{1,0:T(8,128)S(1)}, f32[144,128]{1,0:T(8,128)S(1)}, u32[]{:S(2)}, u32[]{:S(2)}) collective-permute-start(f32[144,128]{1,0:T(8,128)S(1)} %get-tuple-element.5), channel_id=1, source_target_pairs={{0,4},{4,8},{8,12},{12,16},{16,20},{20,24},{24,28},{28,32},{32,36}... | collective-permute-start | bytes 221192 | tf_op jit(solution)/shard_map/ppermute | solution.py:163
  79.5 7.8 %copy-start.1 = (f32[144,128]{1,0:T(8,128)}, f32[144,128]{1,0:T(8,128)S(1)}, u32[]{:S(2)}) copy-start(f32[144,128]{1,0:T(8,128)S(1)} %collective-permute-done.west_ref) | copy-start | bytes 221188
  79.5 7.8 %collective-permute-start.2 = (f32[144,128]{1,0:T(8,128)S(1)}, f32[144,128]{1,0:T(8,128)S(1)}, u32[]{:S(2)}, u32[]{:S(2)}) collective-permute-start(f32[144,128]{1,0:T(8,128)S(1)} %collective-permute-done.west_ref), channel_id=1, source_target_pairs={{0,4},{4,8},{8,12},{12,16},{16,20},{20,24},{24,28},{28,32},{32,36}... | collective-permute-start | bytes 221192 | tf_op jit(solution)/shard_map/ppermute | solution.py:164
  82.1 5.2 %copy-start.2 = (f32[144,128]{1,0:T(8,128)}, f32[144,128]{1,0:T(8,128)S(1)}, u32[]{:S(2)}) copy-start(f32[144,128]{1,0:T(8,128)S(1)} %collective-permute-done.1.north_ref) | copy-start | bytes 221188
  87.3 0.6 copy-start.3

commit v2 on v1

--- a/solution.py
+++ b/solution.py
@@ -1,5 +1,3 @@
-import functools
-
 import jax
 import jax.numpy as jnp
 from jax import lax
@@ -18,6 +16,8 @@
 WIDE = (GROUP_LAT + 2) * LON_DEV
 F32 = jnp.float32
 BF16 = jnp.bfloat16
+MESH = pl.DeviceIdType.MESH
+DEPTH = 512
 
 
 def lanes(rows=1):
@@ -50,16 +50,6 @@
     return one.astype(BF16), two.astype(BF16)
 
 
-def pack_kernel(jac_ref, dep_ref, inv_ref, frac_ref, anch_ref, counts_ref, out_ref):
-    def body(pair, carry):
-        one, two = pack_pair(pair, jac_ref, dep_ref, inv_ref, frac_ref, anch_ref, counts_ref)
-        out_ref[2 * pair] = one
-        out_ref[2 * pair + 1] = two
-        return carry
-
-    lax.fori_loop(0, 64, body, 0)
-
-
 def unpack_pair(one, two):
     left = lanes(HALF) < CAP
     one = one.astype(F32)
@@ -95,27 +85,178 @@
     rhs_ref[(GROUP_LAT + 1) * LON_DEV : (GROUP_LAT + 1) * LON_DEV + 16, cols] = rim.astype(BF16)
 
 
-def sum_kernel(depth, recv_ref, acc_ref, lhs_ref, rhs_ref):
+def place():
+    band, lon = lax.axis_index("band"), lax.axis_index("lon")
+    return lon, band // 8, band // 2 % 4, band % 2
+
+
+def band_of(y, z, core):
+    return (y * 4 + z) * 2 + core
+
+
+def stage_one(n):
+    return n % 4 * (1 - n // 4), (n % 4 + 1) * (n // 4) % 4, n // 7
+
+
+def stage_two(n):
+    return n % 3 + 1, (n // 3 + 1) % 4, n // 9
+
+
+def stage_three(n):
+    return n % 4, n // 4 + 1, 1
+
+
+STAGES = ((stage_one, 0, 8), (stage_two, 8, 12), (stage_three, 20, 12))
+
+
+def main_kernel(
+    jac_hbm, dep_ref, inv_ref, frac_ref, anch_ref, counts_ref,
+    acc_ref, west_out, north_out, corner_out,
+    jac_ref, packed, recv, lhs_ref, rhs_ref, east, south, west, north, corner,
+    jac_sem, own_sem, send_sem, recv_sem, halo_send, halo_recv, x_sem, y_sem, core_sem,
+):
+    x, y, z, core = place()
+    barrier = pltpu.get_barrier_semaphore()
+    x_line = [(band_of(y, z, core), (x + d) % 4) for d in (1, 3, 2)]
+    y_line = [(band_of((y + d) % 4, z, core), x) for d in (1, 3, 2)]
+    z_line = [(band_of(y, (z + d) % 4, core), x) for d in (1, 3, 2)]
+    partner = [(band_of(y, z, 1 - core), x)]
+
+    def greet(sem, devices):
+        for device in devices:
+            pl.semaphore_signal(sem, inc=1, device_id=device, device_id_type=MESH)
+
+    def owner_band(stage, n):
+        dy, dz, dc = stage(n)
+        return band_of((y + dy) % 4, (z + dz) % 4, (core + dc) % 2)
+
+    def pack(stage, base, first, last):
+        def body(n, carry):
+            band = owner_band(stage, n)
+            for half in range(2):
+                one, two = pack_pair(
+                    2 * band + half, jac_ref, dep_ref, inv_ref, frac_ref, anch_ref, counts_ref
+                )
+                packed[(base + n) * 4 + 2 * half] = one
+                packed[(base + n) * 4 + 2 * half + 1] = two
+            return carry
+
+        lax.fori_loop(first, last, body, 0)
+
+    def block_copy(slot, target, source_x, device):
+        return pltpu.make_async_remote_copy(
+            src_ref=packed.at[slot * 4 + target],
+            dst_ref=recv.at[slot * 4 + source_x],
+            send_sem=send_sem.at[slot * 4 + target],
+            recv_sem=recv_sem.at[slot * 4 + source_x],
+            device_id=device,
+            device_id_type=MESH,
+        )
+
+    def send(stage, base, first, last):
+        def body(n, carry):
+            band = owner_band(stage, n)
+            for d in range(4):
+                target = (x + d) % 4
+                block_copy(base + n, target, x, (band, target)).start()
+            return carry
+
+        lax.fori_loop(first, last, body, 0)
+
+    greet(barrier, x_line + y_line + z_line + partner)
+    load = pltpu.make_async_copy(jac_hbm, jac_ref, jac_sem)
+    load.start()
     acc_ref[...] = jnp.zeros_like(acc_ref)
     rhs_ref[...] = jnp.zeros_like(rhs_ref)
+    load.wait()
+    (one, _, _), (two, two_base, _), (three, three_base, _) = STAGES
+    pack(one, 0, 0, 8)
+    pack(two, two_base, 0, 4)
+    pl.semaphore_wait(barrier, 10)
+    greet(x_sem, x_line)
+    pack(two, two_base, 4, 12)
+    pl.semaphore_wait(x_sem, 3)
+    greet(y_sem, y_line)
+    own = pltpu.make_async_copy(packed.at[x], recv.at[x], own_sem)
+    own.start()
+    for d in (1, 3, 2):
+        target = (x + d) % 4
+        block_copy(0, target, x, (band_of(y, z, core), target)).start()
+    send(one, 0, 1, 8)
+    pack(three, three_base, 0, 12)
+    pl.semaphore_wait(y_sem, 3)
+    greet(core_sem, partner)
+    send(two, two_base, 0, 12)
+    pl.semaphore_wait(core_sem, 1)
+    send(three, three_base, 0, 12)
+
+    def arrived(slot, source_x):
+        block_copy(slot, source_x, source_x, x_line[0]).wait_recv()
+
+    own.wait()
+    for d in (1, 3, 2):
+        arrived(0, (x + d) % 4)
 
     def body(step, carry):
-        for n in range(depth // 128):
-            pair = step * (depth // 128) + n
-            spread(unpack_pair(recv_ref[2 * pair], recv_ref[2 * pair + 1]), lhs_ref, rhs_ref, n * 128)
+        for n in range(DEPTH // 256):
+            slot = step * (DEPTH // 256) + n
+
+            @pl.when(slot > 0)
+            def _():
+                for source in range(4):
+                    arrived(slot, source)
+
+            for half in range(2):
+                at = slot * 4 + 2 * half
+                spread(unpack_pair(recv[at], recv[at + 1]), lhs_ref, rhs_ref, n * 256 + half * 128)
         acc_ref[...] += lax.dot_general(
             lhs_ref[...], rhs_ref[...], (((1,), (1,)), ((), ())), preferred_element_type=F32
         )
         return carry
 
-    lax.fori_loop(0, 8192 // depth, body, 0)
-
-
-def halo_of(acc):
-    east = acc[0, :, -LON_DEV:]
+    lax.fori_loop(0, 8192 // DEPTH, body, 0)
+
+    rim = pl.ds(WIDE - LON_DEV, LON_DEV)
+    total = acc_ref[0:ROWS, rim]
     for h in range(1, GROUPS):
-        east = east + jnp.roll(acc[h, :, -LON_DEV:], h * GROUP_LAT, axis=1)
-    return east, acc[GROUPS - 1, :, GROUP_LAT * LON_DEV : (GROUP_LAT + 1) * LON_DEV]
+        total = total + pltpu.roll(acc_ref[h * ROWS : (h + 1) * ROWS, rim], h * GROUP_LAT, 1)
+    east[...] = total
+    south[...] = acc_ref[(GROUPS - 1) * ROWS : GROUPS * ROWS, pl.ds(WIDE - 2 * LON_DEV, LON_DEV)]
+    next_band = (band_of(y, z, core) + 1) % 32
+    halos = []
+    for n, (source, landing, device) in enumerate(
+        [
+            (south, north, (next_band, x)),
+            (east, corner, (next_band, (x + 1) % 4)),
+            (east, west, (band_of(y, z, core), (x + 1) % 4)),
+        ]
+    ):
+        halos.append(
+            pltpu.make_async_remote_copy(
+                src_ref=source,
+                dst_ref=landing,
+                send_sem=halo_send.at[n],
+                recv_sem=halo_recv.at[n],
+                device_id=device,
+                device_id_type=MESH,
+            )
+        )
+    for copy in halos:
+        copy.start()
+
+    def drain(n, carry):
+        slot = n // 4
+        block_copy(slot, n % 4, x, x_line[0]).wait_send()
+        return carry
+
+    for d in (1, 3, 2):
+        block_copy(0, (x + d) % 4, x, x_line[0]).wait_send()
+    lax.fori_loop(4, 128, drain, 0)
+    for copy in halos:
+        copy.wait()
+    west_out[...] = west[...]
+    north_out[...] = north[...]
+    corner_out[...] = corner[...]
 
 
 def final_kernel(acc_ref, west_ref, north_ref, corner_ref, out_ref):
@@ -137,31 +278,39 @@
 
 def per_device(jacobian, departure, inv_var, frac, anchors, counts):
     vmem = pl.BlockSpec(memory_space=pltpu.VMEM)
-    packed = pl.pallas_call(
-        pack_kernel,
-        out_shape=jax.ShapeDtypeStruct((128, HALF, 128), BF16),
-        in_specs=[vmem] * 5 + [pl.BlockSpec(memory_space=pltpu.SMEM)],
-        out_specs=vmem,
-        name="pack",
+    halo = jax.ShapeDtypeStruct((ROWS, LON_DEV), F32)
+    acc, west, north, corner = pl.pallas_call(
+        main_kernel,
+        out_shape=[jax.ShapeDtypeStruct((GROUPS * ROWS, WIDE), F32), halo, halo, halo],
+        in_specs=[pl.BlockSpec(memory_space=pl.ANY)]
+        + [vmem] * 4
+        + [pl.BlockSpec(memory_space=pltpu.SMEM)],
+        out_specs=[vmem] * 4,
+        scratch_shapes=[
+            pltpu.VMEM((LEV, 8192), BF16),
+            pltpu.VMEM((128, HALF, 128), BF16),
+            pltpu.VMEM((128, HALF, 128), BF16),
+            pltpu.VMEM((GROUPS * ROWS, DEPTH), BF16),
+            pltpu.VMEM((WIDE, DEPTH), BF16),
+        ]
+        + [pltpu.VMEM((ROWS, LON_DEV), F32)] * 5
+        + [
+            pltpu.SemaphoreType.DMA,
+            pltpu.SemaphoreType.DMA,
+            pltpu.SemaphoreType.DMA((128,)),
+            pltpu.SemaphoreType.DMA((128,)),
+            pltpu.SemaphoreType.DMA((3,)),
+            pltpu.SemaphoreType.DMA((3,)),
+            pltpu.SemaphoreType.REGULAR,
+            pltpu.SemaphoreType.REGULAR,
+            pltpu.SemaphoreType.REGULAR,
+        ],
+        compiler_params=pltpu.CompilerParams(
+            collective_id=0, has_side_effects=True, vmem_limit_bytes=40 * 2**20
+        ),
+        name="exchange",
     )(jacobian.T, departure.reshape(64, 128), inv_var.reshape(64, 128), frac, anchors, counts)
-    received = lax.all_to_all(packed, ("band", "lon"), split_axis=0, concat_axis=0, tiled=True)
-    depth = 512
-    acc = pl.pallas_call(
-        functools.partial(sum_kernel, depth),
-        out_shape=jax.ShapeDtypeStruct((GROUPS * ROWS, WIDE), F32),
-        in_specs=[vmem],
-        out_specs=vmem,
-        scratch_shapes=[pltpu.VMEM((GROUPS * ROWS, depth), BF16), pltpu.VMEM((WIDE, depth), BF16)],
-        compiler_params=pltpu.CompilerParams(vmem_limit_bytes=40 * 2**20),
-        name="sums",
-    )(received).reshape(GROUPS, ROWS, WIDE)
-    east, south = halo_of(acc)
-    bands, lons = lax.axis_size("band"), lax.axis_size("lon")
-    to_east = [(i, (i + 1) % lons) for i in range(lons)]
-    to_south = [(i, i + 1) for i in range(bands - 1)]
-    west = lax.ppermute(east, "lon", to_east)
-    north = lax.ppermute(south, "band", to_south)
-    corner = lax.ppermute(west, "band", to_south)
+    acc = acc.reshape(GROUPS, ROWS, WIDE)
     block = 48
     out = pl.pallas_call(
         final_kernel,

time: 93.2 us -> 68.7 us (0.74)
  the two profiles are of different devices: /device:TPU:8 before, /device:TPU:1 now
where the time goes in v2:
time: 68.7 us; the launch traced here: 67.5 us
  Pallas kernels  58.5 us (85%)
  local copies, waits for them, and re-layouts  9 us (13%)
    pallas_call x1, Pallas kernels, per_device(): pl.pallas_call(main_kernel, out_shape=[jax.ShapeDtypeStruct((GROUPS * ROW...  53.5 us
    unnamed x20, local copies, waits for them, and re-layouts  9 us
    pallas_call x1, Pallas kernels, per_device(): pl.pallas_call(final_kernel, grid=(ROWS // block,), out_shape=jax.ShapeDt...  4.94 us

profile of v2, /device:TPU:1, one launch (start us, length us, event | category | flops | bytes accessed | tf_op | source)
XLA Modules:
  0.0 67.5 jit_solution(2964282408484937258)
XLA Ops:
  0.0 0.0 copy-start.1
  0.0 1.7 %copy-done.1 = bf16[8192,137]{0,1:T(8,128)(2,1)S(1)} copy-done((bf16[8192,137]{0,1:T(8,128)(2,1)S(1)}, bf16[8192,137]{0,1:T(8,128)(2,1)}, u32[]{:S(2)}) %copy-start.1) | copy-done | bytes 2244632
  1.7 0.0 copy-start.5
  1.7 0.8 %copy-done.5 = f32[2,8192]{1,0:T(2,128)S(1)} copy-done((f32[2,8192]{1,0:T(2,128)S(1)}, f32[2,8192]{1,0:T(2,128)}, u32[]{:S(2)}) %copy-start.5) | copy-done | bytes 65560
  2.5 0.0 copy-start.6
  2.5 0.8 %copy-done.6 = s32[2,8192]{1,0:T(2,128)S(1)} copy-done((s32[2,8192]{1,0:T(2,128)S(1)}, s32[2,8192]{1,0:T(2,128)}, u32[]{:S(2)}) %copy-start.6) | copy-done | bytes 65560
  3.3 0.0 copy-start.7
  3.3 0.8 %copy-done.7 = f32[8192]{0:T(1024)S(1)} copy-done((f32[8192]{0:T(1024)S(1)}, f32[8192]{0:T(1024)}, u32[]{:S(2)}) %copy-start.7) | copy-done | bytes 32792
  4.1 0.0 copy-start.8
  4.1 0.8 %copy-done.8 = f32[8192]{0:T(1024)S(1)} copy-done((f32[8192]{0:T(1024)S(1)}, f32[8192]{0:T(1024)}, u32[]{:S(2)}) %copy-start.8) | copy-done | bytes 32792
  4.9 0.0 copy-start.9
  4.9 0.7 copy-done.9
  5.5 53.5 %exchange.1 = (f32[576,1280]{1,0:T(8,128)S(1)}, f32[144,128]{1,0:T(8,128)S(1)}, f32[144,128]{1,0:T(8,128)S(1)}, f32[144,128]{1,0:T(8,128)S(1)}) custom-call(bf16[137,8192]{1,0:T(8,128)(2,1)S(1)} %bitcast.6, f32[64,128]{1,0:T(8,128)S(1)} %bitcast.7, f32[64,128]{1,0:T(8,128)S(1)} %bitcast.8, f32[2,8192]{1,0:T(2,128)S(1)} %copy-done.5, ...), custom_call_target="tpu_custom_call" | custom-call | tf_op jit(solution)/shard_map/exchange/pallas_call | solution.py:282
  59.1 0.0 copy-start
  59.1 1.6 %copy-done = f32[576,1280]{1,0:T(8,128)} copy-done((f32[576,1280]{1,0:T(8,128)}, f32[576,1280]{1,0:T(8,128)S(1)}, u32[]{:S(2)}) %copy-start) | copy-done | bytes 2949144
  60.7 0.0 copy-start.2
  60.7 0.6 copy-done.2
  61.3 0.0 copy-start.3
  61.3 0.6 copy-done.3
  61.9 0.0 copy-start.4
  61.9 0.6 copy-done.4
  62.6 4.9 %final.1 = f32[4384,128]{1,0:T(8,128)} custom-call(f32[4,144,1280]{2,1,0:T(8,128)} %bitcast.5, f32[144,128]{1,0:T(8,128)} %copy-done.2, f32[144,128]{1,0:T(8,128)} %copy-done.3, f32[144,128]{1,0:T(8,128)} %copy-done.4), custom_call_target="tpu_custom_call" | custom-call | tf_op jit(solution)/shard_map/final/pallas_call | solution.py:315
Async XLA Ops:
  0.0 1.7 %copy-start.1 = (bf16[8192,137]{0,1:T(8,128)(2,1)S(1)}, bf16[8192,137]{0,1:T(8,128)(2,1)}, u32[]{:S(2)}) copy-start(bf16[8192,137]{0,1:T(8,128)(2,1)} %param.6) | copy-start | bytes 6733828
  1.7 0.8 %copy-start.5 = (f32[2,8192]{1,0:T(2,128)S(1)}, f32[2,8192]{1,0:T(2,128)}, u32[]{:S(2)}) copy-start(f32[2,8192]{1,0:T(2,128)} %frac_ref.1) | copy-start | bytes 196612
  2.5 0.8 %copy-start.6 = (s32[2,8192]{1,0:T(2,128)S(1)}, s32[2,8192]{1,0:T(2,128)}, u32[]{:S(2)}) copy-start(s32[2,8192]{1,0:T(2,128)} %anch_ref.1) | copy-start | bytes 196612
  3.3 0.8 %copy-start.7 = (f32[8192]{0:T(1024)S(1)}, f32[8192]{0:T(1024)}, u32[]{:S(2)}) copy-start(f32[8192]{0:T(1024)} %param.7) | copy-start | bytes 98308
  4.1 0.8 %copy-start.8 = (f32[8192]{0:T(1024)S(1)}, f32[8192]{0:T(1024)}, u32[]{:S(2)}) copy-start(f32[8192]{0:T(1024)} %param.8) | copy-start | bytes 98308
  4.9 0.7 copy-start.9
  59.1 1.6 %copy-start = (f32[576,1280]{1,0:T(8,128)}, f32[576,1280]{1,0:T(8,128)S(1)}, u32[]{:S(2)}) copy-start(f32[576,1280]{1,0:T(8,128)S(1)} %get-tuple-element.9) | copy-start | bytes 8847364
  60.7 0.6 copy-start.2
  61.3 0.6 copy-start.3
  61.9 0.6 copy-start.4

commit v3 on v2

v3 whole, which is shorter than its diff:
```python
import jax
import jax.numpy as jnp
from jax import lax
from jax.experimental import pallas as pl
from jax.experimental.pallas import tpu as pltpu
from jax.sharding import PartitionSpec as P

LEV = 137
LAT_DEV = 32
LON_DEV = 128
CAP = 64
ROWS = 144
HALF = ROWS // 2
GROUPS = 4
GROUP_LAT = LAT_DEV // GROUPS
WIDE = (GROUP_LAT + 2) * LON_DEV
F32 = jnp.float32
BF16 = jnp.bfloat16
MESH = pl.DeviceIdType.MESH
DEPTH = 256
BLOCKS = DEPTH // CAP


def lanes(rows=1):
    return lax.broadcasted_iota(jnp.int32, (rows, 128), 1)


def pack_pair(pair, jac_ref, dep_ref, inv_ref, frac_ref, anch_ref, counts_ref):
    cols = pl.ds(pl.multiple_of(pair * 128, 128), 128)
    lane = lanes()
    first = lane < CAP
    limit = jnp.where(first, counts_ref[0, 2 * pair], counts_ref[0, 2 * pair + 1])
    live = (lane % CAP) < limit
    forcing = dep_ref[pl.ds(pair, 1), :] * inv_ref[pl.ds(pair, 1), :]
    top = jnp.where(live, jac_ref[0:136, cols].astype(F32) * forcing, 0.0)
    last = jnp.where(live, jac_ref[136:137, cols].astype(F32) * forcing, 0.0)
    a = frac_ref[0:1, cols]
    b = frac_ref[1:2, cols]
    lat = (anch_ref[0:1, cols] % LAT_DEV).astype(F32)
    lon = (anch_ref[1:2, cols] % LON_DEV).astype(F32)
    items = [last, (1.0 - a) * (1.0 - b), (1.0 - a) * b, a * (1.0 - b), a * b, lat, lon]
    row = lax.broadcasted_iota(jnp.int32, (8, 128), 0)
    tail = jnp.zeros((8, 128), F32)
    for n, item in enumerate(items):
        tail = jnp.where((row == n) & live, item, tail)
    low = top[0:HALF]
    high = jnp.concatenate([top[HALF:136], tail], axis=0)
    left = lanes(HALF) < CAP
    one = jnp.where(left, low, pltpu.roll(high, CAP, 1))
    two = jnp.where(left, pltpu.roll(low, CAP, 1), high)
    return one.astype(BF16), two.astype(BF16)


def unpack_pair(one, two):
    left = lanes(HALF) < CAP
    one = one.astype(F32)
    two = two.astype(F32)
    low = jnp.where(left, one, pltpu.roll(two, CAP, 1))
    high = jnp.where(left, pltpu.roll(one, CAP, 1), two)
    return jnp.concatenate([low, high], axis=0)


def spread(slots, lhs_ref, rhs_ref, at):
    cols = pl.ds(at, 128)
    info = slots[136:144]
    w00, w01, w10, w11 = (info[n : n + 1] for n in range(1, 5))
    lat, lon = info[5:6], info[6:7]
    group = jnp.floor(lat * (1.0 / GROUP_LAT))
    inner = lat - group * GROUP_LAT
    adj = slots.astype(BF16)
    for h in range(GROUPS):
        mask = jnp.where(group == h, 1.0, 0.0).astype(BF16)
        lhs_ref[h * ROWS : (h + 1) * ROWS, cols] = adj * mask
    j = lax.broadcasted_iota(jnp.int32, (LON_DEV, 128), 0).astype(F32)
    here = j == lon
    after = j == lon + 1.0
    near = jnp.where(here, w00, jnp.where(after, w01, 0.0)).astype(BF16)
    far = jnp.where(here, w10, jnp.where(after, w11, 0.0)).astype(BF16)
    for r in range(GROUP_LAT + 1):
        on_near = jnp.where(inner == r, 1.0, 0.0).astype(BF16)
        on_far = jnp.where(inner + 1.0 == r, 1.0, 0.0).astype(BF16)
        rhs_ref[r * LON_DEV : (r + 1) * LON_DEV, cols] = near * on_near + far * on_far
    edge = lon == LON_DEV - 1.0
    r = lax.broadcasted_iota(jnp.int32, (16, 128), 0).astype(F32)
    rim = jnp.where(edge & (r == inner), w01, jnp.where(edge & (r == inner + 1.0), w11, 0.0))
    rhs_ref[(GROUP_LAT + 1) * LON_DEV : (GROUP_LAT + 1) * LON_DEV + 16, cols] = rim.astype(BF16)


def place():
    band, lon = lax.axis_index("band"), lax.axis_index("lon")
    return lon, band // 8, band // 2 % 4, band % 2


def band_of(y, z, core):
    return (y * 4 + z) * 2 + core


ORDER = (
    (0, 0, 0, 0, 0),
    (0, 0, 0, 1, 1),
    (2, 2, 0, 0, 5),
    (2, 3, 0, 0, 4),
    (0, 1, 0, 0, 6),
    (3, 2, 0, 0, 8),
    (1, 0, 0, 0, 2),
    (1, 2, 0, 0, 10),
    (3, 0, 0, 0, 3),
    (2, 1, 0, 0, 12),
    (0, 3, 0, 0, 7),
    (1, 1, 0, 0, 11),
    (3, 3, 0, 0, 9),
    (3, 1, 0, 0, 16),
    (1, 3, 0, 0, 13),
    (2, 0, 0, 0, 14),
    (0, 2, 0, 0, 15),
    (0, 0, 2, 0, 98),
    (0, 0, 3, 0, 85),
    (0, 0, 1, 0, 91),
    (2, 2, 2, 0, 20),
    (3, 2, 2, 0, 19),
    (1, 0, 2, 0, 17),
    (1, 2, 2, 0, 21),
    (3, 0, 2, 0, 18),
    (2, 3, 2, 0, 23),
    (0, 1, 2, 0, 37),
    (2, 1, 2, 0, 26),
    (0, 3, 2, 0, 95),
    (3, 3, 2, 0, 22),
    (1, 1, 2, 0, 24),
    (3, 1, 2, 0, 27),
    (1, 3, 2, 0, 28),
    (2, 2, 3, 0, 30),
    (2, 2, 1, 0, 31),
    (0, 2, 2, 0, 48),
    (2, 0, 2, 0, 35),
    (2, 3, 3, 0, 33),
    (0, 1, 1, 0, 64),
    (2, 1, 1, 0, 32),
    (0, 3, 3, 0, 92),
    (1, 2, 3, 0, 39),
    (3, 0, 1, 0, 25),
    (3, 2, 1, 0, 38),
    (1, 0, 3, 0, 29),
    (2, 3, 1, 0, 40),
    (0, 1, 3, 0, 82),
    (3, 2, 3, 0, 41),
    (1, 0, 1, 0, 34),
    (2, 1, 3, 0, 44),
    (0, 3, 1, 0, 94),
    (1, 2, 1, 0, 43),
    (3, 0, 3, 0, 36),
    (1, 1, 1, 0, 42),
    (3, 3, 3, 0, 45),
    (1, 1, 3, 0, 51),
    (3, 3, 1, 0, 46),
    (0, 2, 3, 0, 63),
    (2, 0, 1, 0, 47),
    (1, 3, 3, 0, 52),
    (3, 1, 1, 0, 50),
    (3, 1, 3, 0, 55),
    (1, 3, 1, 0, 54),
    (2, 0, 3, 0, 56),
    (0, 2, 1, 0, 74),
    (2, 2, 2, 1, 60),
    (2, 2, 3, 1, 58),
    (0, 0, 1, 1, 109),
    (2, 1, 2, 1, 61),
    (0, 3, 0, 1, 90),
    (1, 2, 2, 1, 66),
    (3, 0, 0, 1, 49),
    (2, 2, 1, 1, 62),
    (0, 0, 3, 1, 96),
    (2, 3, 2, 1, 68),
    (0, 1, 0, 1, 87),
    (3, 2, 2, 1, 69),
    (1, 0, 0, 1, 53),
    (1, 2, 1, 1, 75),
    (3, 0, 3, 1, 59),
    (2, 3, 3, 1, 70),
    (0, 1, 1, 1, 108),
    (0, 2, 2, 1, 111),
    (2, 0, 0, 1, 57),
    (2, 2, 0, 1, 67),
    (0, 0, 2, 1, 126),
    (2, 1, 1, 1, 71),
    (0, 3, 3, 1, 93),
    (2, 0, 2, 1, 78),
    (0, 2, 0, 1, 110),
    (2, 1, 3, 1, 77),
    (0, 3, 1, 1, 112),
    (1, 1, 2, 1, 79),
    (3, 3, 0, 1, 65),
    (3, 2, 3, 1, 84),
    (1, 0, 1, 1, 72),
    (2, 3, 1, 1, 81),
    (0, 1, 3, 1, 113),
    (1, 2, 3, 1, 88),
    (3, 0, 1, 1, 73),
    (3, 2, 1, 1, 89),
    (1, 0, 3, 1, 80),
    (3, 3, 2, 1, 99),
    (1, 1, 0, 1, 76),
    (1, 3, 2, 1, 102),
    (3, 1, 0, 1, 83),
    (3, 1, 2, 1, 104),
    (1, 3, 0, 1, 86),
    (3, 3, 3, 1, 101),
    (1, 1, 1, 1, 100),
    (1, 0, 2, 1, 105),
    (3, 2, 0, 1, 97),
    (0, 2, 3, 1, 114),
    (2, 0, 1, 1, 103),
    (1, 1, 3, 1, 107),
    (3, 3, 1, 1, 106),
    (0, 2, 1, 1, 117),
    (2, 0, 3, 1, 118),
    (2, 3, 0, 1, 115),
    (0, 1, 2, 1, 123),
    (3, 1, 3, 1, 119),
    (1, 3, 1, 1, 121),
    (0, 3, 2, 1, 127),
    (2, 1, 0, 1, 116),
    (3, 1, 1, 1, 122),
    (1, 3, 3, 1, 124),
    (3, 0, 2, 1, 125),
    (1, 2, 0, 1, 120),
)


def main_kernel(
    jac_hbm, dep_hbm, inv_hbm, frac_hbm, anch_hbm, counts_hbm,
    out_ref,
    jac_ref, dep_ref, inv_ref, frac_ref, anch_ref, counts_ref, acc_ref, packed, recv, lhs_even, rhs_even, lhs_odd, rhs_odd, east, south, west, north, corner,
    load_sem, own_sem, send_sem, recv_sem, halo_send, halo_recv, z_sem, core_sem,
):
    x, y, z, core = place()
    barrier = pltpu.get_barrier_semaphore()
    plane = [
        (band_of((y + dy) % 4, z, core), (x + dx) % 4)
        for dx, dy in sorted({(n % 4, n // 4) for n in range(1, 16)})
    ]
    z_line = [(band_of(y, (z + d) % 4, core), x) for d in (1, 3, 2)]
    partner = [(band_of(y, z, 1 - core), x)]

    def greet(sem, devices):
        for device in devices:
            pl.semaphore_signal(sem, inc=1, device_id=device, device_id_type=MESH)

    def pack(first, last):
        def body(n, carry):
            band = band_of((y + n) % 4, (z + n // 4) % 4, (core + n // 16) % 2)
            for half in range(2):
                one, two = pack_pair(
                    2 * band + half, jac_ref, dep_ref, inv_ref, frac_ref, anch_ref, counts_ref
                )
                packed[n * 4 + 2 * half] = one
                packed[n * 4 + 2 * half + 1] = two
            return carry

        lax.fori_loop(first, last, body, 0)

    def block_copy(n):
        dx, dy, dz, dc, slot = ORDER[n]
        target = (x + dx) % 4
        return pltpu.make_async_remote_copy(
            src_ref=packed.at[(dc * 16 + dz * 4 + dy) * 4 + target],
            dst_ref=recv.at[slot],
            send_sem=send_sem.at[slot],
            recv_sem=recv_sem.at[slot],
            device_id=(band_of((y + dy) % 4, (z + dz) % 4, (core + dc) % 2), target),
            device_id_type=MESH,
        )

    def send(first, last):
        for n in range(first, last):
            block_copy(n).start()

    greet(barrier, plane + z_line + partner)
    loads = [
        pltpu.make_async_copy(source, held, load_sem.at[n])
        for n, (source, held) in enumerate(
            [
                (counts_hbm, counts_ref),
                (dep_hbm, dep_ref),
                (inv_hbm, inv_ref),
                (frac_hbm, frac_ref),
                (anch_hbm, anch_ref),
                (jac_hbm, jac_ref),
            ]
        )
    ]
    for load in loads:
        load.start()
    acc_ref[...] = jnp.zeros_like(acc_ref)
    for held in (rhs_even, rhs_odd):
        held[...] = jnp.zeros_like(held)
    for load in loads:
        load.wait()
    pack(0, 17)
    pl.semaphore_wait(barrier, 19)
    greet(z_sem, z_line)
    send(1, 17)
    pack(17, 22)
    pl.semaphore_wait(z_sem, 3)
    greet(core_sem, partner)
    send(17, 65)
    pl.semaphore_wait(core_sem, 1)
    pack(22, 32)
    own = pltpu.make_async_copy(packed.at[x], recv.at[0], own_sem)
    own.start()
    send(65, 128)

    def arrived(slot):
        pltpu.make_async_remote_copy(
            src_ref=packed.at[slot],
            dst_ref=recv.at[slot],
            send_sem=send_sem.at[slot],
            recv_sem=recv_sem.at[slot],
            device_id=partner[0],
            device_id_type=MESH,
        ).wait_recv()

    def fill(step, lhs_ref, rhs_ref, first=0):
        for n in range(first, BLOCKS):
            arrived(step * BLOCKS + n)
        for n in range(0, BLOCKS, 2):
            at = step * BLOCKS + n
            spread(unpack_pair(recv[at], recv[at + 1]), lhs_ref, rhs_ref, n * CAP)

    def add(lhs_ref, rhs_ref):
        acc_ref[...] += lax.dot_general(
            lhs_ref[...], rhs_ref[...], (((1,), (1,)), ((), ())), preferred_element_type=F32
        )

    own.wait()
    fill(0, lhs_even, rhs_even, 1)

    def body(t, carry):
        fill(2 * t + 1, lhs_odd, rhs_odd)
        add(lhs_even, rhs_even)
        fill(2 * t + 2, lhs_even, rhs_even)
        add(lhs_odd, rhs_odd)
        return carry

    lax.fori_loop(0, 8192 // DEPTH // 2 - 1, body, 0)
    add(lhs_even, rhs_even)
    fill(8192 // DEPTH - 1, lhs_odd, rhs_odd)
    add(lhs_odd, rhs_odd)

    rim = pl.ds(WIDE - LON_DEV, LON_DEV)
    total = acc_ref[0:ROWS, rim]
    for h in range(1, GROUPS):
        total = total + pltpu.roll(acc_ref[h * ROWS : (h + 1) * ROWS, rim], h * GROUP_LAT, 1)
    east[...] = total
    south[...] = acc_ref[(GROUPS - 1) * ROWS : GROUPS * ROWS, pl.ds(WIDE - 2 * LON_DEV, LON_DEV)]
    next_band = (band_of(y, z, core) + 1) % 32
    halos = []
    for n, (source, landing, device) in enumerate(
        [
            (south, north, (next_band, x)),
            (east, corner, (next_band, (x + 1) % 4)),
            (east, west, (band_of(y, z, core), (x + 1) % 4)),
        ]
    ):
        halos.append(
            pltpu.make_async_remote_copy(
                src_ref=source,
                dst_ref=landing,
                send_sem=halo_send.at[n],
                recv_sem=halo_recv.at[n],
                device_id=device,
                device_id_type=MESH,
            )
        )
    for copy in halos:
        copy.start()

    def own_row(i):
        h, r = i // GROUP_LAT, i % GROUP_LAT
        value = acc_ref[h * ROWS : (h + 1) * ROWS, r * LON_DEV : (r + 1) * LON_DEV]
        if r == 0 and h > 0:
            value = value + acc_ref[
                (h - 1) * ROWS : h * ROWS, GROUP_LAT * LON_DEV : (GROUP_LAT + 1) * LON_DEV
            ]
        return value

    def drain(slot, carry):
        pltpu.make_async_remote_copy(
            src_ref=packed.at[slot],
            dst_ref=recv.at[slot],
            send_sem=send_sem.at[slot],
            recv_sem=recv_sem.at[slot],
            device_id=partner[0],
            device_id_type=MESH,
        ).wait_send()
        return carry

    lax.fori_loop(1, 128, drain, 0)
    for copy in halos:
        copy.wait()
    lane = lanes(LEV)
    for i in range(LAT_DEV):
        value = own_row(i)[0:LEV]
        side = west[0:LEV, i : i + 1]
        if i == 0:
            value = value + north[0:LEV]
            side = side + corner[0:LEV, LAT_DEV : LAT_DEV + 1]
        out_ref[pl.ds(i, LEV, stride=LAT_DEV), :] = value + jnp.where(lane == 0, side, 0.0)


def per_device(jacobian, departure, inv_var, frac, anchors, counts):
    out = pl.pallas_call(
        main_kernel,
        out_shape=jax.ShapeDtypeStruct((LEV * LAT_DEV, LON_DEV), F32),
        in_specs=[pl.BlockSpec(memory_space=pltpu.HBM)] * 6,
        out_specs=pl.BlockSpec(memory_space=pltpu.VMEM),
        scratch_shapes=[
            pltpu.VMEM((LEV, 8192), BF16),
            pltpu.VMEM((64, 128), F32),
            pltpu.VMEM((64, 128), F32),
            pltpu.VMEM((2, 8192), F32),
            pltpu.VMEM((2, 8192), jnp.int32),
            pltpu.SMEM((1, 128), jnp.int32),
            pltpu.VMEM((GROUPS * ROWS, WIDE), F32),
            pltpu.VMEM((128, HALF, 128), BF16),
            pltpu.VMEM((128, HALF, 128), BF16),
            pltpu.VMEM((GROUPS * ROWS, DEPTH), BF16),
            pltpu.VMEM((WIDE, DEPTH), BF16),
            pltpu.VMEM((GROUPS * ROWS, DEPTH), BF16),
            pltpu.VMEM((WIDE, DEPTH), BF16),
        ]
        + [pltpu.VMEM((ROWS, LON_DEV), F32)] * 5
        + [
            pltpu.SemaphoreType.DMA((6,)),
            pltpu.SemaphoreType.DMA,
            pltpu.SemaphoreType.DMA((128,)),
            pltpu.SemaphoreType.DMA((128,)),
            pltpu.SemaphoreType.DMA((3,)),
            pltpu.SemaphoreType.DMA((3,)),
            pltpu.SemaphoreType.REGULAR,
            pltpu.SemaphoreType.REGULAR,
        ],
        compiler_params=pltpu.CompilerParams(
            collective_id=0, has_side_effects=True, vmem_limit_bytes=40 * 2**20
        ),
        name="exchange",
    )(
        *(
            pltpu.with_memory_space_constraint(value, pltpu.HBM)
            for value in (
                jacobian.T,
                departure.reshape(64, 128),
                inv_var.reshape(64, 128),
                frac,
                anchors,
                counts,
            )
        )
    )
    return out.reshape(LEV, LAT_DEV, LON_DEV)


def solution(mesh):
    return jax.shard_map(
        per_device,
        mesh=mesh,
        in_specs=(
            P(("band", "lon"), None),
            P(("band", "lon")),
            P(("band", "lon")),
            P(None, ("band", "lon")),
            P(None, ("band", "lon")),
            P(("band", "lon"), None),
        ),
        out_specs=P(None, "band", "lon"),
        check_vma=False,
    )
```

time: 68.7 us -> 56.1 us (0.82); the launches traced: 67.5 us -> 55.9 us
  local copies, waits for them, and re-layouts: 9 us -> 1.37 us
  Pallas kernels: 58.5 us -> 54.6 us
    unnamed x20 -> x1, local copies, waits for them, and re-layouts: 9 us -> 1.37 us
    pallas_call x2 -> x1, Pallas kernels: 58.5 us -> 54.6 us  [per_device(): pl.pallas_call(main_kernel, out_shape=jax.ShapeDtypeStruct((LEV * LAT_DEV...]
where the time goes in v3:
time: 56.1 us; the launch traced here: 55.9 us
  Pallas kernels  54.6 us (97%)
  local copies, waits for them, and re-layouts  1.37 us (2%)
    pallas_call x1, Pallas kernels, per_device(): pl.pallas_call(main_kernel, out_shape=jax.ShapeDtypeStruct((LEV * LAT_DEV...  54.6 us
    unnamed x1, local copies, waits for them, and re-layouts  1.37 us

profile of v3, /device:TPU:1, one launch (start us, length us, event | category | flops | bytes accessed | tf_op | source)
XLA Modules:
  0.0 55.9 jit_solution(162884886277694114)
XLA Ops:
  0.0 54.6 %exchange.1 = f32[4384,128]{1,0:T(8,128)S(1)} custom-call(bf16[137,8192]{1,0:T(8,128)(2,1)} %bitcast.5, f32[64,128]{1,0:T(8,128)} %bitcast.6, f32[64,128]{1,0:T(8,128)} %bitcast.7, f32[2,8192]{1,0:T(2,128)} %frac_hbm.1, s32[2,8192]{1,0:T(2,128)} %anch_hbm.1, s32[1,128]{1,0:T(1,128)} %counts_hbm.1), custom_call_target="tpu_custom_call" | custom-call | tf_op jit(solution)/shard_map/exchange/pallas_call | solution.py:412
  54.6 1.4 %copy.8 = f32[137,32,128]{2,1,0:T(8,128)} copy(f32[137,32,128]{2,1,0:T(8,128)S(1)} %bitcast.4) | data formatting | bytes 4489216

commit v4 on v3

--- a/solution.py
+++ b/solution.py
@@ -17,8 +17,11 @@
 F32 = jnp.float32
 BF16 = jnp.bfloat16
 MESH = pl.DeviceIdType.MESH
+CONTRACT = (((1,), (1,)), ((), ()))
 DEPTH = 256
 BLOCKS = DEPTH // CAP
+LATE = 512
+EDGE = GROUP_LAT * LON_DEV
 
 
 def lanes(rows=1):
@@ -230,7 +233,7 @@
 def main_kernel(
     jac_hbm, dep_hbm, inv_hbm, frac_hbm, anch_hbm, counts_hbm,
     out_ref,
-    jac_ref, dep_ref, inv_ref, frac_ref, anch_ref, counts_ref, acc_ref, packed, recv, lhs_even, rhs_even, lhs_odd, rhs_odd, east, south, west, north, corner,
+    jac_ref, dep_ref, inv_ref, frac_ref, anch_ref, counts_ref, acc_ref, packed, recv, lhs_even, rhs_even, lhs_odd, rhs_odd, lhs_late, rhs_late, east, south, west, north, corner,
     load_sem, own_sem, send_sem, recv_sem, halo_send, halo_recv, z_sem, core_sem,
 ):
     x, y, z, core = place()
@@ -292,8 +295,8 @@
     for load in loads:
         load.start()
     acc_ref[...] = jnp.zeros_like(acc_ref)
-    for held in (rhs_even, rhs_odd):
-        held[...] = jnp.zeros_like(held)
+    for held in (rhs_even, rhs_odd, rhs_late):
+        held[EDGE + LON_DEV : WIDE, :] = jnp.zeros((LON_DEV, held.shape[1]), BF16)
     for load in loads:
         load.wait()
     pack(0, 17)
@@ -329,11 +332,12 @@
 
     def add(lhs_ref, rhs_ref):
         acc_ref[...] += lax.dot_general(
-            lhs_ref[...], rhs_ref[...], (((1,), (1,)), ((), ())), preferred_element_type=F32
+            lhs_ref[...], rhs_ref[...], CONTRACT, preferred_element_type=F32
         )
 
     own.wait()
     fill(0, lhs_even, rhs_even, 1)
+    early = (8192 - LATE) // DEPTH
 
     def body(t, carry):
         fill(2 * t + 1, lhs_odd, rhs_odd)
@@ -342,10 +346,30 @@
         add(lhs_odd, rhs_odd)
         return carry
 
-    lax.fori_loop(0, 8192 // DEPTH // 2 - 1, body, 0)
+    lax.fori_loop(0, early // 2 - 1, body, 0)
     add(lhs_even, rhs_even)
-    fill(8192 // DEPTH - 1, lhs_odd, rhs_odd)
+    fill(early - 1, lhs_odd, rhs_odd)
     add(lhs_odd, rhs_odd)
+
+    def collect(step, carry):
+        for n in range(4):
+            arrived(early * BLOCKS + step * 4 + n)
+        for n in range(0, 4, 2):
+            at = early * BLOCKS + step * 4 + n
+            column = pl.multiple_of((step * 4 + n) * CAP, 128)
+            spread(unpack_pair(recv[at], recv[at + 1]), lhs_late, rhs_late, column)
+        return carry
+
+    lax.fori_loop(0, LATE // CAP // 4, collect, 0)
+
+    def late(n, carry):
+        cols = pl.ds(pl.multiple_of(n * 256, 256), 256)
+        acc_ref[:, cols] += lax.dot_general(
+            lhs_late[...], rhs_late[cols, :], CONTRACT, preferred_element_type=F32
+        )
+        return carry
+
+    lax.fori_loop(EDGE // 256, EDGE // 256 + 1, late, 0)
 
     rim = pl.ds(WIDE - LON_DEV, LON_DEV)
     total = acc_ref[0:ROWS, rim]
@@ -384,6 +408,10 @@
             ]
         return value
 
+    lax.fori_loop(0, EDGE // 256, late, 0)
+    for i in range(LAT_DEV):
+        out_ref[pl.ds(i, LEV, stride=LAT_DEV), :] = own_row(i)[0:LEV]
+
     def drain(slot, carry):
         pltpu.make_async_remote_copy(
             src_ref=packed.at[slot],
@@ -398,14 +426,14 @@
     lax.fori_loop(1, 128, drain, 0)
     for copy in halos:
         copy.wait()
-    lane = lanes(LEV)
-    for i in range(LAT_DEV):
-        value = own_row(i)[0:LEV]
-        side = west[0:LEV, i : i + 1]
-        if i == 0:
-            value = value + north[0:LEV]
-            side = side + corner[0:LEV, LAT_DEV : LAT_DEV + 1]
-        out_ref[pl.ds(i, LEV, stride=LAT_DEV), :] = value + jnp.where(lane == 0, side, 0.0)
+    top = pl.ds(0, LEV, stride=LAT_DEV)
+    side = jnp.where(lanes(LEV) == 0, corner[0:LEV, LAT_DEV : LAT_DEV + 1], 0.0)
+    out_ref[top, :] += north[0:LEV] + side
+    columns = jnp.transpose(west[...])[0:LAT_DEV]
+    first = lanes(LAT_DEV) == 0
+    for level in range(LEV):
+        rows = pl.ds(level * LAT_DEV, LAT_DEV)
+        out_ref[rows, :] += jnp.where(first, columns[:, level : level + 1], 0.0)
 
 
 def per_device(jacobian, departure, inv_var, frac, anchors, counts):
@@ -428,6 +456,8 @@
             pltpu.VMEM((WIDE, DEPTH), BF16),
             pltpu.VMEM((GROUPS * ROWS, DEPTH), BF16),
             pltpu.VMEM((WIDE, DEPTH), BF16),
+            pltpu.VMEM((GROUPS * ROWS, LATE), BF16),
+            pltpu.VMEM((WIDE, LATE), BF16),
         ]
         + [pltpu.VMEM((ROWS, LON_DEV), F32)] * 5
         + [

time: 56.1 us -> 54.7 us (0.975)
  Pallas kernels: 54.6 us -> 53.2 us
    pallas_call x1, Pallas kernels: 54.6 us -> 53.2 us  [per_device(): pl.pallas_call(main_kernel, out_shape=jax.ShapeDtypeStruct((LEV * LAT_DEV...]
where the time goes in v4:
time: 54.7 us; the launch traced here: 54.6 us
  Pallas kernels  53.2 us (97%)
  local copies, waits for them, and re-layouts  1.37 us (3%)
    pallas_call x1, Pallas kernels, per_device(): pl.pallas_call(main_kernel, out_shape=jax.ShapeDtypeStruct((LEV * LAT_DEV...  53.2 us
    unnamed x1, local copies, waits for them, and re-layouts  1.37 us

profile of v4, /device:TPU:1, one launch (start us, length us, event | category | flops | bytes accessed | tf_op | source)
XLA Modules:
  0.0 54.6 jit_solution(1354230120601789117)
XLA Ops:
  0.0 53.2 %exchange.1 = f32[4384,128]{1,0:T(8,128)S(1)} custom-call(bf16[137,8192]{1,0:T(8,128)(2,1)} %bitcast.5, f32[64,128]{1,0:T(8,128)} %bitcast.6, f32[64,128]{1,0:T(8,128)} %bitcast.7, f32[2,8192]{1,0:T(2,128)} %frac_hbm.1, s32[2,8192]{1,0:T(2,128)} %anch_hbm.1, s32[1,128]{1,0:T(1,128)} %counts_hbm.1), custom_call_target="tpu_custom_call" | custom-call | tf_op jit(solution)/shard_map/exchange/pallas_call | solution.py:440
  53.2 1.4 %copy.8 = f32[137,32,128]{2,1,0:T(8,128)} copy(f32[137,32,128]{2,1,0:T(8,128)S(1)} %bitcast.4) | data formatting | bytes 4489216

commit v5 on v4

--- a/solution.py
+++ b/solution.py
@@ -307,8 +307,8 @@
     pl.semaphore_wait(z_sem, 3)
     greet(core_sem, partner)
     send(17, 65)
+    pack(22, 32)
     pl.semaphore_wait(core_sem, 1)
-    pack(22, 32)
     own = pltpu.make_async_copy(packed.at[x], recv.at[0], own_sem)
     own.start()
     send(65, 128)

time: 54.7 us -> 55 us (level)
  no operation moved by 1% of the time
where the time goes in v5:
time: 55 us; the launch traced here: 54.6 us
  Pallas kernels  53.2 us (97%)
  local copies, waits for them, and re-layouts  1.37 us (2%)
    pallas_call x1, Pallas kernels, per_device(): pl.pallas_call(main_kernel, out_shape=jax.ShapeDtypeStruct((LEV * LAT_DEV...  53.2 us
    unnamed x1, local copies, waits for them, and re-layouts  1.37 us

profile of v5, /device:TPU:1, one launch (start us, length us, event | category | flops | bytes accessed | tf_op | source)
XLA Modules:
  0.0 54.6 jit_solution(5610658791702874134)
XLA Ops:
  0.0 53.2 %exchange.1 = f32[4384,128]{1,0:T(8,128)S(1)} custom-call(bf16[137,8192]{1,0:T(8,128)(2,1)} %bitcast.5, f32[64,128]{1,0:T(8,128)} %bitcast.6, f32[64,128]{1,0:T(8,128)} %bitcast.7, f32[2,8192]{1,0:T(2,128)} %frac_hbm.1, s32[2,8192]{1,0:T(2,128)} %anch_hbm.1, s32[1,128]{1,0:T(1,128)} %counts_hbm.1), custom_call_target="tpu_custom_call" | custom-call | tf_op jit(solution)/shard_map/exchange/pallas_call | solution.py:440
  53.2 1.4 %copy.8 = f32[137,32,128]{2,1,0:T(8,128)} copy(f32[137,32,128]{2,1,0:T(8,128)S(1)} %bitcast.4) | data formatting | bytes 4489216
